TPU v7x, 512 devices: a whole 4x8x8 slice. The times are simulated.
512 devices in a mesh: dp: 4 (over x), expert: 128 (over y, z, core).
Axes of the slice: x: 4, y: 8, z: 8, core: 2. Of those that a mesh axis runs over, the one named last changes fastest.
Arguments:
- tokens: bfloat16 [16384, 2048], P('expert', 'dp'), may hold values from -6 to 6
- expert_ids: int32 [16384, 8], P('expert'), may hold values from 0 to 127, all different within a row; in each aligned block of 128 rows (0 to 127, 128 to 255, ...) at most 12 rows name the same one
- chosen_probs: float32 [16384, 8], P('expert'), may hold values from 0.05 to 1
- gate_weight: bfloat16 [128, 1536, 2048], P('expert', 'dp'), may hold values from -0.125 to 0.125
- up_weight: bfloat16 [128, 1536, 2048], P('expert', 'dp'), may hold values from -0.125 to 0.125
- down_weight: bfloat16 [128, 1536, 2048], P('expert', 'dp'), may hold values from -0.15625 to 0.15625
Outputs:
- mixed: bfloat16 [16384, 2048], P('expert', 'dp')
Inputs may be any that keep to these rules, and one draw needn't show every extreme that they name: `expert_ids`: each row names 8 different experts; the 128 rows of one device name each expert at most 12 times, a bound that some block reaches.
All inputs are finite; a program needn't handle non-finite values.
Results may differ from a plain program's by a relative error of at most 0.0058.
Values may be sent and summed in bfloat16 or wider, within the bound.
A program may use at most 128 MiB of HBM per device.

v0:
```python
import jax
import jax.numpy as jnp
from jax import lax
from jax.sharding import PartitionSpec as P


def local(tokens, expert_ids, chosen_probs, gate_weight, up_weight, down_weight):
    n_experts = lax.axis_size("expert")
    tok_rows = expert_ids.shape[0]
    top_count = expert_ids.shape[1]
    capacity = min(
        tok_rows, max(2, (3 * tok_rows * top_count + 2 * n_experts - 1) // (2 * n_experts))
    )
    route = chosen_probs / jnp.sum(chosen_probs, axis=1, keepdims=True)
    flat = expert_ids.reshape(-1)
    onehot = (flat[:, None] == jnp.arange(n_experts, dtype=jnp.int32)[None, :]).astype(jnp.int32)
    slot = jnp.sum(onehot * (jnp.cumsum(onehot, axis=0) - 1), axis=1)
    place = flat * capacity + slot
    tok_index = jnp.arange(tok_rows * top_count, dtype=jnp.int32) // top_count
    source = lax.all_gather(tokens, "dp", axis=1, tiled=True)
    columns_now = source.shape[1]
    buffer = (
        jnp.zeros((n_experts * capacity, columns_now), jnp.bfloat16)
        .at[place]
        .set(source[tok_index])
    )
    outgoing = buffer.reshape(n_experts, capacity, columns_now)
    gate_local = gate_weight[0]
    up_local = up_weight[0]
    down_local = down_weight[0]
    arrived = lax.all_to_all(outgoing, "expert", split_axis=0, concat_axis=0, tiled=True)
    gate = jnp.einsum("snd,fd->snf", arrived, gate_local, preferred_element_type=jnp.float32)
    up = jnp.einsum("snd,fd->snf", arrived, up_local, preferred_element_type=jnp.float32)
    hidden = (jax.nn.silu(gate) * up).astype(jnp.bfloat16)
    produced = jnp.einsum(
        "snf,fd->snd", hidden, down_local, preferred_element_type=jnp.float32
    ).astype(jnp.bfloat16)
    returned = lax.all_to_all(produced, "expert", split_axis=0, concat_axis=0, tiled=True)
    width = returned.shape[2]
    picked = returned.reshape(n_experts * capacity, width)[place]
    weighted = picked.astype(jnp.float32) * route.reshape(-1)[:, None]
    partial_out = jnp.sum(weighted.reshape(tok_rows, top_count, width), axis=1)
    return lax.psum_scatter(partial_out, "dp", scatter_dimension=1, tiled=True).astype(jnp.bfloat16)


def solution(mesh):
    in_specs = (
        P("expert", "dp"),
        P("expert", None),
        P("expert", None),
        P("expert", "dp", None),
        P("expert", "dp", None),
        P("expert", "dp", None),
    )
    out_specs = P("expert", "dp")
    return jax.shard_map(local, mesh=mesh, in_specs=in_specs, out_specs=out_specs, check_vma=False)
```

profile of v0, /device:TPU:1, one launch (start us, length us, event | category | flops | bytes accessed | tf_op | source)
XLA Modules:
  0.0 663.5 jit_solution(5687706592367524285)
XLA Ops:
  6.5 0.0 copy-start
  6.5 0.9 copy.17
  7.4 0.1 eq.29
  7.5 0.1 eq.25
  7.6 0.7 broadcast_multiply_fusion
  8.3 0.1 copy.19
  8.4 0.2 fusion.19
  8.7 0.1 copy.20
  8.8 0.1 copy.16
  8.9 0.1 mul.37
  9.0 11.3 %all_gather.3 = bf16[128,2048]{1,0:T(8,128)(2,1)S(1)} all-gather(bf16[128,512]{1,0:T(8,128)(2,1)} %param.6), channel_id=1, replica_groups=mesh['dp'=4,'expert'=128] {'dp'}, dimensions={1}, use_global_device_ids=true | all-gather | bytes 655360 | tf_op jit(solution)/shard_map/all_gather | solution.py:20
  20.3 0.4 fusion.18
  20.7 34.5 %scatter_custom_fusion = bf16[1536,2048]{1,0:T(8,128)(2,1)} fusion(s32[1024]{0:T(1024)S(1)} %bitcast.29, bf16[128,2048]{1,0:T(8,128)(2,1)S(1)} %all_gather.3, s32[1024]{0:T(1024)S(1)} %broadcast_clamp_fusion.1, bf16[]{:T(256)} %constant.28.clone.1), kind=kCustom, calls=%fused_computation.10 | custom fusion | bytes 6291458 | tf_op jit(solution)/shard_map/scatter | solution.py:25
  55.2 10.6 %reshape.109 = bf16[128,12,2048]{2,1,0:T(8,128)(2,1)} reshape(bf16[1536,2048]{1,0:T(8,128)(2,1)} %scatter_custom_fusion) | data formatting | bytes 12582912 | tf_op jit(solution)/shard_map/reshape | solution.py:27
  65.8 0.0 copy-start.4
  65.8 212.0 %all_to_all.10 = bf16[128,12,2048]{2,1,0:T(8,128)(2,1)S(1)} all-to-all(bf16[128,12,2048]{2,1,0:T(8,128)(2,1)} %reshape.109), channel_id=1, replica_groups=mesh['dp'=4,'expert'=128] {'expert'}, dimensions={0} | all-to-all | bytes 12582912 | tf_op jit(solution)/shard_map/all_to_all | solution.py:31
  277.8 0.0 copy-start.2
  277.8 3.3 copy-done.2
  281.2 0.0 copy-done.4
  281.2 9.0 %fusion.3 = f32[128,12,384]{2,0,1:T(8,128)} fusion(bf16[128,12,2048]{2,1,0:T(8,128)(2,1)S(1)} %all_to_all.10, bf16[1,384,2048]{2,1,0:T(8,128)(2,1)S(1)} %copy-done.4), kind=kOutput, calls=%fused_computation.8 | convolution fusion | flops 2415919104 | bytes 10223616 | tf_op jit(solution)/shard_map/snd,fd->snf/dot_general | solution.py:32
  290.1 0.0 copy-done
  290.1 14.2 %convolution_convert_fusion = bf16[128,12,2048]{2,0,1:T(8,128)(2,1)} fusion(bf16[1,384,2048]{2,1,0:T(8,128)(2,1)S(1)} %copy-done, f32[128,12,384]{2,0,1:T(8,128)} %fusion.3, bf16[128,12,2048]{2,1,0:T(8,128)(2,1)} %copy-done.2, bf16[1,384,2048]{2,1,0:T(8,128)(2,1)} %param.10), kind=kOutput, calls=%fused_computation.5 | convolution fusion | flops 4838522880 | bytes 18087936 | tf_op jit(solution)/shard_map/snf,fd->snd/dot_general | solution.py:35
  304.3 9.6 %copy.23 = bf16[128,12,2048]{2,1,0:T(8,128)(2,1)} copy(bf16[128,12,2048]{2,0,1:T(8,128)(2,1)} %convolution_convert_fusion) | data formatting | bytes 12582912 | tf_op jit(solution)/shard_map/convert_element_type | solution.py:37
  314.0 0.0 copy-start.3
  314.0 20.4 %all-to-all-start.1 = ((bf16[128,12,2048]{2,1,0:T(8,128)(2,1)}), bf16[128,12,2048]{2,1,0:T(8,128)(2,1)}, u32[]{:S(2)}, u32[]{:S(2)}) async-start(bf16[128,12,2048]{2,1,0:T(8,128)(2,1)} %copy.23), calls=%async_computation.1 | async-start | bytes 16777216 | tf_op jit(solution)/shard_map/all_to_all | solution.py:38
  334.4 0.0 reduce-scatter.2.cloned.1.call-start
  334.4 0.0 copy-done.3
  334.5 0.1 copy.24
  334.6 225.2 %all-to-all-done.1 = bf16[128,12,2048]{2,1,0:T(8,128)(2,1)} async-done(((bf16[128,12,2048]{2,1,0:T(8,128)(2,1)}), bf16[128,12,2048]{2,1,0:T(8,128)(2,1)}, u32[]{:S(2)}, u32[]{:S(2)}) %all-to-all-start.1) | async-done | bytes 6291488 | tf_op jit(solution)/shard_map/all_to_all | solution.py:38
  559.8 10.9 %reshape.110 = bf16[1536,2048]{1,0:T(8,128)(2,1)} reshape(bf16[128,12,2048]{2,1,0:T(8,128)(2,1)} %all-to-all-done.1) | data formatting | bytes 12582912 | tf_op jit(solution)/shard_map/reshape | solution.py:40
  570.7 0.0 copy-start.1
  570.7 12.5 %gather_fusion = bf16[1024,2048]{1,0:T(8,128)(2,1)} fusion(bf16[1536,2048]{1,0:T(8,128)(2,1)} %reshape.110, s32[1024]{0:T(1024)S(1)} %broadcast_clamp_fusion), kind=kCustom, calls=%fused_computation.1 | custom fusion | bytes 8392704 | tf_op jit(solution)/shard_map/gather | solution.py:40
  583.3 7.5 %fusion = f32[128,2048]{1,0:T(8,128)} fusion(bf16[1024,2048]{1,0:T(8,128)(2,1)} %gather_fusion, f32[128,8]{1,0:T(8,128)S(1)} %copy.24), kind=kLoop, calls=%fused_computation.4 | loop fusion | flops 6029312 | bytes 5246976 | tf_op jit(solution)/shard_map/reduce_sum | solution.py:42
  590.7 0.0 reduce-scatter.2.cloned.1.call-update
  590.7 63.8 %reduce-scatter.2.cloned.1.call-done = f32[128,512]{1,0:T(8,128)} async-done(((f32[128,2048]{1,0:T(8,128)}), f32[128,512]{1,0:T(8,128)}) %reduce-scatter.2.cloned.1.call-update) | async-done | bytes 262160 | tf_op jit(solution)/shard_map/reduce_scatter | solution.py:43
  654.5 1.6 convert_element_type.26
  656.2 0.0 copy-done.1
  (10 shorter events, 0.1 us)
Async XLA Ops:
  6.5 283.6 %copy-start = (bf16[1,384,2048]{2,1,0:T(8,128)(2,1)S(1)}, bf16[1,384,2048]{2,1,0:T(8,128)(2,1)}, u32[]{:S(2)}) copy-start(bf16[1,384,2048]{2,1,0:T(8,128)(2,1)} %param.11) | copy-start | bytes 4718596
  65.8 215.3 %copy-start.4 = (bf16[1,384,2048]{2,1,0:T(8,128)(2,1)S(1)}, bf16[1,384,2048]{2,1,0:T(8,128)(2,1)}, u32[]{:S(2)}) copy-start(bf16[1,384,2048]{2,1,0:T(8,128)(2,1)} %param.9) | copy-start | bytes 4718596
  277.8 3.3 copy-start.2
  314.0 20.5 %copy-start.3 = (f32[128,8]{0,1:T(8,128)S(1)}, f32[128,8]{0,1:T(8,128)}, u32[]{:S(2)}) copy-start(f32[128,8]{0,1:T(8,128)} %param.8) | copy-start | bytes 12292
  314.0 245.8 %all-to-all-start.1 = ((bf16[128,12,2048]{2,1,0:T(8,128)(2,1)}), bf16[128,12,2048]{2,1,0:T(8,128)(2,1)}, u32[]{:S(2)}, u32[]{:S(2)}) async-start(bf16[128,12,2048]{2,1,0:T(8,128)(2,1)} %copy.23), calls=%async_computation.1 | async-start | bytes 16777216 | tf_op jit(solution)/shard_map/all_to_all | solution.py:38
  334.4 320.2 %reduce-scatter.2.cloned.1.call-start = ((), (), s32[]{:S(2)}) async-start(), calls=%async_computation.3 | async-start | bytes 1310720 | tf_op jit(solution)/shard_map/reduce_scatter | solution.py:43
  570.7 85.5 %copy-start.1 = (bf16[1,384,2048]{2,1,0:T(8,128)(2,1)S(1)}, bf16[1,384,2048]{2,1,0:T(8,128)(2,1)}, u32[]{:S(2)}) copy-start(bf16[1,384,2048]{2,1,0:T(8,128)(2,1)} %param.11) | copy-start | bytes 4718596
Sparse Core Ops, SparseCore 0:
  590.9 63.6 reduce-scatter.1
where the time goes:
time: 669 us; the launch traced here: 663 us
  waiting for transfers between devices  289 us (43%)
  blocking collectives  223 us (33%)
  local copies, waits for them, and re-layouts  83.2 us (12%)
  matrix products  23.1 us (3%)
  starting transfers between devices  20.5 us (3%)
  between operations  13.9 us (2%)
  other arithmetic  10.4 us (2%)
    all_to_all x1, waiting for transfers between devices, local(): lax.all_to_all(produced, 'expert', split_axis=0, concat_axis=0, tiled=True)  225 us
    all_to_all x1, blocking collectives, local(): lax.all_to_all(outgoing, 'expert', split_axis=0, concat_axis=0, tiled=True)  212 us
    reduce_scatter x1, waiting for transfers between devices, local(): lax.psum_scatter(partial_out, 'dp', scatter_dimension=1, tiled=True)  63.8 us
    scatter x1, local copies, waits for them, and re-layouts, local(): buffer = jnp.zeros((n_experts * capacity, columns_now), jnp.bfloat16).at[...  34.5 us
    all_to_all x1, starting transfers between devices, local(): lax.all_to_all(produced, 'expert', split_axis=0, concat_axis=0, tiled=True)  20.4 us
    dot_general x1, matrix products, local(): jnp.einsum('snf,fd->snd', hidden, down_local, preferred_element_type=jnp....  14.2 us
  transfers between devices with their start and end apart: 2, of which 2 were waited for; matrix products, arithmetic and copies ran while one was open for 0% of the time, Pallas kernels for 0%

commit v1 on v0

v1 whole, which is shorter than its diff:
```python
import functools

import jax
import jax.numpy as jnp
from jax import lax
from jax.experimental import pallas as pl
from jax.experimental.pallas import tpu as pltpu
from jax.sharding import PartitionSpec as P

LANES = 128
CAP = 12
TILE = 16
TILES = 3
ROWS = TILE * TILES
F32 = jnp.float32
BF16 = jnp.bfloat16


def wanted_slot(tile, row):
    return jnp.where(row < CAP, row, row - CAP + 4 * tile)


def pack_kernel(ids_ref, tok_ref, out_ref):
    tokens = tok_ref.shape[0]
    experts = out_ref.shape[0]
    which = lax.broadcasted_iota(jnp.int32, (experts, tokens), 0)
    chosen = jnp.zeros((experts, tokens), F32)
    for k in range(ids_ref.shape[0]):
        chosen = chosen + (which == ids_ref[k : k + 1, :]).astype(F32)
    before = lax.broadcasted_iota(jnp.int32, (tokens, tokens), 0)
    after = lax.broadcasted_iota(jnp.int32, (tokens, tokens), 1)
    upper = (before < after).astype(F32).astype(BF16)
    rank = jnp.dot(chosen.astype(BF16), upper, preferred_element_type=F32)
    slot = jnp.where(chosen > 0.0, rank, -1.0).astype(jnp.int32)
    block = min(16, experts)
    row = lax.broadcasted_iota(jnp.int32, (block, TILE, tokens), 1)
    rows2 = lax.broadcasted_iota(jnp.int32, (block, TILE, LANES), 1)
    for start in range(0, experts, block):
        mine = jnp.broadcast_to(slot[start : start + block][:, None, :], (block, TILE, tokens))
        for tile in range(TILES):
            pick = (mine == wanted_slot(tile, row)).astype(F32).astype(BF16)
            pick = pick.reshape(block * TILE, tokens)
            source = jnp.concatenate(
                [tok_ref[:, tile * LANES : (tile + 1) * LANES], tok_ref[:, TILES * LANES :]], axis=1
            )
            got = jnp.dot(pick, source, preferred_element_type=F32)
            main = got[:, :LANES].reshape(block, TILE, LANES)
            rest = got[:, LANES:].reshape(block, TILE, LANES)
            out_ref[start : start + block, tile * TILE : (tile + 1) * TILE, :] = jnp.where(
                rows2 < CAP, main, rest
            ).astype(BF16)


def grid_place(nz):
    e = lax.axis_index("expert")
    core = lax.rem(e, 2)
    z = lax.rem(lax.div(e, 2), nz)
    y = lax.div(e, 2 * nz)
    return e, y, z, core


def peer_of(k, sign, place, ny, nz):
    _, y, z, core = place
    group = lax.div(k, 2 * nz)
    item = lax.rem(k, 2 * nz)
    dz = lax.div(item, 2)
    dc = lax.rem(item, 2)
    dy = lax.rem(dz + group, ny)
    if sign > 0:
        y2, z2 = lax.rem(y + dy, ny), lax.rem(z + dz, nz)
    else:
        y2, z2 = lax.rem(y + ny - dy, ny), lax.rem(z + nz - dz, nz)
    return (y2 * nz + z2) * 2 + lax.rem(core + dc, 2)


def remote(src, dst, send, recv, device):
    return pltpu.make_async_remote_copy(
        src_ref=src,
        dst_ref=dst,
        send_sem=send,
        recv_sem=recv,
        device_id=device,
        device_id_type=pl.DeviceIdType.MESH,
    )


def enter(place, n, ny, nz, right, left):
    barrier = pltpu.get_barrier_semaphore()

    def greet(k, carry):
        pl.semaphore_signal(
            barrier,
            inc=1,
            device_id={"expert": peer_of(k, 1, place, ny, nz)},
            device_id_type=pl.DeviceIdType.MESH,
        )
        return carry

    lax.fori_loop(1, n, greet, 0)
    for side in (right, left):
        pl.semaphore_signal(
            barrier, inc=1, device_id={"dp": side}, device_id_type=pl.DeviceIdType.MESH
        )
    pl.semaphore_wait(barrier, n + 1)


def dispatch_kernel(ny, nz, packed, out, own_sem, send_sem, recv_sem, xsend, lsem, rsem, fsem):
    n = 2 * ny * nz
    per = 2 * nz
    x = lax.axis_index("dp")
    place = grid_place(nz)
    e = place[0]
    right, left = lax.rem(x + 1, 4), lax.rem(x + 3, 4)
    enter(place, n, ny, nz, right, left)

    own = pltpu.make_async_copy(packed.at[e], out.at[x, 0], own_sem)
    own.start()
    for g in range(ny):

        def send(k, carry, g=g):
            dest = peer_of(k, 1, place, ny, nz)
            remote(
                packed.at[dest], out.at[x, k], send_sem, recv_sem.at[g], {"expert": dest}
            ).start()
            return carry

        lax.fori_loop(max(1, g * per), (g + 1) * per, send, 0)
    own.wait()

    def part(q, g):
        return out.at[q, pl.ds(g * per, per)]

    def forward(g):
        if g % 2 == 0:
            remote(part(left, g), part(left, g), xsend, lsem.at[g], {"dp": right}).wait_recv()
            remote(part(left, g), part(left, g), xsend, fsem.at[g], {"dp": right}).start()
        else:
            remote(part(right, g), part(right, g), xsend, rsem.at[g], {"dp": left}).wait_recv()
            remote(part(right, g), part(right, g), xsend, fsem.at[g], {"dp": left}).start()

    for g in range(ny):
        first = 1 if g == 0 else 0
        whole = out.at[x, pl.ds(g * per + first, per - first)]
        remote(whole, whole, send_sem, recv_sem.at[g], {"dp": right}).wait_recv()
        remote(part(x, g), part(x, g), xsend, lsem.at[g], {"dp": right}).start()
        remote(part(x, g), part(x, g), xsend, rsem.at[g], {"dp": left}).start()
        if g >= 1:
            forward(g - 1)
    forward(ny - 1)
    far = lax.rem(x + 2, 4)
    for g in range(ny):
        if g % 2 == 0:
            remote(part(right, g), part(right, g), xsend, rsem.at[g], {"dp": left}).wait_recv()
        else:
            remote(part(left, g), part(left, g), xsend, lsem.at[g], {"dp": right}).wait_recv()
        remote(part(far, g), part(far, g), xsend, fsem.at[g], {"dp": right}).wait_recv()
    sent = packed.at[pl.ds(0, n - 1)]
    remote(sent, sent, send_sem, recv_sem.at[0], {"dp": right}).wait_send()
    three = out.at[pl.ds(0, 3)]
    remote(three, three, xsend, recv_sem.at[0], {"dp": right}).wait_send()


def expert_kernel(in_ref, gate_ref, up_ref, down_ref, out_ref, rows_ref):
    parts, batch = in_ref.shape[0], in_ref.shape[1]
    rows = batch * TILE
    half = TILE // 2
    low = lax.broadcasted_iota(jnp.int32, (batch, half, LANES), 1) < half // 2
    for q in range(parts):
        uppers = []
        base = q * (TILES + 1) * LANES
        for tile in range(TILES):
            value = in_ref[q, :, tile * TILE : (tile + 1) * TILE, :]
            rows_ref[:, base + tile * LANES : base + (tile + 1) * LANES] = value.reshape(rows, LANES)
            uppers.append(value.astype(F32)[:, half:, :])
        first = jnp.where(low, pltpu.roll(uppers[0], half // 2, 1), uppers[1])
        second = pltpu.roll(uppers[2], half // 2, 1)
        last = jnp.concatenate([first, second], axis=1).reshape(rows, LANES).astype(BF16)
        rows_ref[:, base + TILES * LANES : base + (TILES + 1) * LANES] = last
    dims = (((1,), (1,)), ((), ()))
    gate = lax.dot_general(rows_ref[...], gate_ref[0], dims, preferred_element_type=F32)
    up = lax.dot_general(rows_ref[...], up_ref[0], dims, preferred_element_type=F32)
    hidden = (gate / (1.0 + jnp.exp(-gate)) * up).astype(BF16)
    for q in range(parts):
        base = q * (TILES + 1) * LANES
        made = jnp.dot(
            hidden, down_ref[0, :, base : base + (TILES + 1) * LANES], preferred_element_type=F32
        )
        last = made[:, TILES * LANES :].reshape(batch, TILE, LANES)
        fill = (
            pltpu.roll(last[:, :half], half // 2, 1),
            last[:, :half],
            pltpu.roll(last[:, half:], half // 2, 1),
        )
        for tile in range(TILES):
            main = made[:, tile * LANES : (tile + 1) * LANES].reshape(batch, TILE, LANES)
            upper = jnp.where(low, main[:, half:], fill[tile])
            out_ref[q, :, tile * TILE : (tile + 1) * TILE, :] = jnp.concatenate(
                [main[:, :half], upper], axis=1
            ).astype(BF16)


def return_kernel(
    ny, nz, made, ret,
    own, near, diag, from_left, from_right, passed, total,
    own_sem, near_sem, dsem, lsem, rsem, xsend, send_sem, ret_sem, last_sem,
):
    n = 2 * ny * nz
    per = 2 * nz
    x = lax.axis_index("dp")
    place = grid_place(nz)
    e = place[0]
    right, left, far = lax.rem(x + 1, 4), lax.rem(x + 3, 4), lax.rem(x + 2, 4)

    def part(q, g):
        return made.at[q, pl.ds(g * per, per)]

    def stage_own(g):
        return pltpu.make_async_copy(part(x, g), own.at[g], own_sem.at[g])

    def stage_near(g):
        side = right if g % 2 == 0 else left
        return pltpu.make_async_copy(part(side, g), near.at[g], near_sem.at[g])

    for g in range(ny):
        stage_near(g).start()
        stage_own(g).start()
    enter(place, n, ny, nz, right, left)

    def issue(g):
        if g % 2 == 0:
            remote(part(far, g), diag.at[g], xsend, dsem.at[g], {"dp": right}).start()
            remote(part(left, g), from_right.at[g], xsend, rsem.at[g], {"dp": left}).start()
        else:
            remote(part(far, g), diag.at[g], xsend, dsem.at[g], {"dp": left}).start()
            remote(part(right, g), from_left.at[g], xsend, lsem.at[g], {"dp": right}).start()

    def forward(g):
        stage_near(g).wait()
        remote(diag.at[g], diag.at[g], xsend, dsem.at[g], {"dp": right}).wait_recv()
        passed[g] = (diag[g].astype(F32) + near[g].astype(F32)).astype(BF16)
        if g % 2 == 0:
            remote(passed.at[g], from_left.at[g], xsend, lsem.at[g], {"dp": right}).start()
        else:
            remote(passed.at[g], from_right.at[g], xsend, rsem.at[g], {"dp": left}).start()

    def finish(g):
        stage_own(g).wait()
        remote(from_left.at[g], from_left.at[g], xsend, lsem.at[g], {"dp": right}).wait_recv()
        remote(from_right.at[g], from_right.at[g], xsend, rsem.at[g], {"dp": right}).wait_recv()
        total[g] = (
            own[g].astype(F32) + from_left[g].astype(F32) + from_right[g].astype(F32)
        ).astype(BF16)

        def send(i, carry):
            dest = peer_of(g * per + i, -1, place, ny, nz)
            remote(total.at[g, i], ret.at[e], send_sem, ret_sem, {"expert": dest}).start()
            return carry

        lax.fori_loop(1 if g == 0 else 0, per, send, 0)
        if g == 0:
            pltpu.make_async_copy(total.at[0, 0], ret.at[e], last_sem).start()

    ahead = min(ny, 4)
    for g in range(ahead):
        issue(g)
    for g in range(0, ny, 2):
        forward(g)
        forward(g + 1)
        for h in (g + ahead, g + ahead + 1):
            if h < ny:
                issue(h)
        if g >= 2:
            finish(g - 2)
            finish(g - 1)
    finish(ny - 2)
    finish(ny - 1)
    pltpu.make_async_copy(total.at[0, 0], ret.at[e], last_sem).wait()
    most = ret.at[pl.ds(0, n - 1)]
    remote(most, most, send_sem, ret_sem, {"dp": right}).wait()
    three = made.at[pl.ds(0, 3)]
    remote(three, three, xsend, ret_sem, {"dp": right}).wait_send()


def combine_kernel(ids_ref, probs_ref, ret_ref, out_ref):
    tokens, top = ids_ref.shape
    experts = ret_ref.shape[0]
    probs = probs_ref[...]
    route = probs / jnp.sum(probs, axis=1, keepdims=True)
    ids = ids_ref[...]
    which = lax.broadcasted_iota(jnp.int32, (tokens, experts), 1)
    chosen = jnp.zeros((tokens, experts), F32)
    weight = jnp.zeros((tokens, experts), F32)
    for k in range(top):
        hit = which == ids[:, k : k + 1]
        chosen = chosen + hit.astype(F32)
        weight = weight + jnp.where(hit, route[:, k : k + 1], 0.0)
    here = lax.broadcasted_iota(jnp.int32, (tokens, tokens), 0)
    other = lax.broadcasted_iota(jnp.int32, (tokens, tokens), 1)
    lower = (other < here).astype(F32).astype(BF16)
    rank = jnp.dot(lower, chosen.astype(BF16), preferred_element_type=F32)
    slot = jnp.where(chosen > 0.0, rank, -1.0).astype(BF16)
    high = weight.astype(BF16)
    rest = (weight - high.astype(F32)).astype(BF16)
    wide = experts * TILE
    column = lax.broadcasted_iota(jnp.int32, (experts, wide), 1)
    line = lax.broadcasted_iota(jnp.int32, (experts, wide), 0)
    spread = ((column >= line * TILE) & (column < line * TILE + TILE)).astype(F32).astype(BF16)
    slots = jnp.dot(slot, spread, preferred_element_type=F32).astype(jnp.int32)
    highs = jnp.dot(high, spread, preferred_element_type=F32)
    rests = jnp.dot(rest, spread, preferred_element_type=F32)
    row = lax.broadcasted_iota(jnp.int32, (tokens, wide), 1) & (TILE - 1)
    last = jnp.zeros((tokens, LANES), F32)
    for tile in range(TILES):
        hit = slots == wanted_slot(tile, row)
        masks = (hit & (row < CAP), hit & (row >= CAP))
        left = jnp.concatenate(
            [jnp.where(m, w, 0.0).astype(BF16) for m in masks for w in (highs, rests)], axis=0
        )
        right = ret_ref[:, tile * TILE : (tile + 1) * TILE, :].reshape(wide, LANES)
        got = jnp.dot(left, right, preferred_element_type=F32)
        out_ref[:, tile * LANES : (tile + 1) * LANES] = (
            got[:tokens] + got[tokens : 2 * tokens]
        ).astype(BF16)
        last = last + got[2 * tokens : 3 * tokens] + got[3 * tokens :]
    out_ref[:, TILES * LANES :] = last.astype(BF16)


def vmem(count):
    return [pl.BlockSpec(memory_space=pltpu.VMEM)] * count


ANYWHERE = pl.BlockSpec(memory_space=pl.ANY)


def local(ny, nz, tokens, expert_ids, chosen_probs, gate_weight, up_weight, down_weight):
    n = 2 * ny * nz
    per = 2 * nz
    dma = pltpu.SemaphoreType.DMA
    packed = pl.pallas_call(
        pack_kernel,
        out_shape=jax.ShapeDtypeStruct((n, ROWS, LANES), BF16),
        in_specs=vmem(2),
        out_specs=vmem(1)[0],
        name="pack",
    )(expert_ids.T, tokens)
    arrived = pl.pallas_call(
        functools.partial(dispatch_kernel, ny, nz),
        out_shape=jax.ShapeDtypeStruct((4, n, ROWS, LANES), BF16),
        in_specs=[ANYWHERE],
        out_specs=ANYWHERE,
        scratch_shapes=[
            dma(()), dma(()), dma((ny,)), dma(()), dma((ny,)), dma((ny,)), dma((ny,)),
        ],
        compiler_params=pltpu.CompilerParams(collective_id=0, has_side_effects=True),
        name="dispatch",
    )(packed)
    ff, width = gate_weight.shape[1], gate_weight.shape[2]
    batch = min(32, n)
    block = pl.BlockSpec((4, batch, ROWS, LANES), lambda i: (0, i, 0, 0))
    whole = pl.BlockSpec((1, ff, width), lambda i: (0, 0, 0), pipeline_mode=pl.Buffered(1))
    made = pl.pallas_call(
        expert_kernel,
        grid=(n // batch,),
        out_shape=jax.ShapeDtypeStruct((4, n, ROWS, LANES), BF16),
        in_specs=[block, whole, whole, whole],
        out_specs=block,
        scratch_shapes=[pltpu.VMEM((batch * TILE, width), BF16)],
        name="expert",
    )(arrived, gate_weight, up_weight, down_weight)
    held = pltpu.VMEM((ny, per, ROWS, LANES), BF16)
    back = pl.pallas_call(
        functools.partial(return_kernel, ny, nz),
        out_shape=jax.ShapeDtypeStruct((n, ROWS, LANES), BF16),
        in_specs=[ANYWHERE],
        out_specs=ANYWHERE,
        scratch_shapes=[held] * 7
        + [dma((ny,))] * 5
        + [dma(()), dma(()), dma(()), dma(())],
        compiler_params=pltpu.CompilerParams(collective_id=1, has_side_effects=True),
        name="giveback",
    )(made)
    return pl.pallas_call(
        combine_kernel,
        out_shape=jax.ShapeDtypeStruct(tokens.shape, BF16),
        in_specs=vmem(3),
        out_specs=vmem(1)[0],
        name="combine",
    )(expert_ids, chosen_probs, back)


def build(mesh, ny, nz):
    in_specs = (
        P("expert", "dp"),
        P("expert", None),
        P("expert", None),
        P("expert", "dp", None),
        P("expert", "dp", None),
        P("expert", "dp", None),
    )
    return jax.shard_map(
        functools.partial(local, ny, nz),
        mesh=mesh,
        in_specs=in_specs,
        out_specs=P("expert", "dp"),
        check_vma=False,
    )


def solution(mesh):
    return build(mesh, 8, 8)
```

time: 669 us -> 196 us (0.29)
  waiting for transfers between devices: 289 us -> 0 us
  blocking collectives: 223 us -> 0 us
  Pallas kernels: 0 us -> 193 us
  local copies, waits for them, and re-layouts: 83.2 us -> 1.44 us
  matrix products: 23.1 us -> 0 us
  starting transfers between devices: 20.5 us -> 0 us
  between operations: 13.9 us -> 0.03 us
  other arithmetic: 10.4 us -> 0 us
    all_to_all x1 -> x0, waiting for transfers between devices: 225 us -> none  [local(): lax.all_to_all(produced, 'expert', split_axis=0, concat_axis=0, tiled=True)]
    all_to_all x1 -> x0, blocking collectives: 212 us -> none  [local(): lax.all_to_all(outgoing, 'expert', split_axis=0, concat_axis=0, tiled=True)]
    pallas_call x0 -> x5, Pallas kernels: none -> 193 us  [the longest x1 84.1 us: local(): pl.pallas_call(functools.partial(dispatch_kernel, ny, nz), out_shape=jax....]
    reduce_scatter x1 -> x0, waiting for transfers between devices: 63.8 us -> none  [local(): lax.psum_scatter(partial_out, 'dp', scatter_dimension=1, tiled=True)]
    scatter x1 -> x0, local copies, waits for them, and re-layouts: 34.5 us -> none  [local(): buffer = jnp.zeros((n_experts * capacity, columns_now), jnp.bfloat16).at[...]
    dot_general x2 -> x0, matrix products: 23.1 us -> none  [the longest x1 14.2 us: local(): jnp.einsum('snf,fd->snd', hidden, down_local, preferred_element_type=jnp....]
    reshape x2 -> x0, local copies, waits for them, and re-layouts: 21.5 us -> none  [the longest x1 10.9 us: local(): picked = returned.reshape(n_experts * capacity, width)[place]]
    all_to_all x1 -> x0, starting transfers between devices: 20.4 us -> none  [local(): lax.all_to_all(produced, 'expert', split_axis=0, concat_axis=0, tiled=True)]
  transfers between devices with their start and end apart: 2 -> 0, of which waited for: 2 -> 0; matrix products, arithmetic and copies ran while one was open for 0% -> 0% of each run, Pallas kernels for 0% -> 0%
where the time goes in v1:
time: 196 us; the launch traced here: 195 us
  Pallas kernels  193 us (98%)
    pallas_call x1, Pallas kernels, local(): pl.pallas_call(functools.partial(dispatch_kernel, ny, nz), out_shape=jax....  84.1 us
    pallas_call x1, Pallas kernels, local(): pl.pallas_call(functools.partial(return_kernel, ny, nz), out_shape=jax.Sh...  82.5 us
    pallas_call x1, Pallas kernels, local(): pl.pallas_call(expert_kernel, grid=(n // batch,), out_shape=jax.ShapeDtyp...  17.9 us
    pallas_call x1, Pallas kernels, local(): pl.pallas_call(combine_kernel, out_shape=jax.ShapeDtypeStruct(tokens.shap...  5.63 us

profile of v1, /device:TPU:1, one launch (start us, length us, event | category | flops | bytes accessed | tf_op | source)
XLA Modules:
  0.0 194.9 jit_solution(6259399372987434469)
XLA Ops:
  0.0 3.2 %pack.1.packed = bf16[128,48,128]{2,1,0:T(8,128)(2,1)} custom-call(s32[8,128]{1,0:T(8,128)} %bitcast.1, bf16[128,512]{1,0:T(8,128)(2,1)} %tok_ref.1), custom_call_target="tpu_custom_call" | custom-call | tf_op jit(solution)/shard_map/pack/pallas_call | solution.py:339
  3.2 84.1 %dispatch.1.in_ref = bf16[4,128,48,128]{3,2,1,0:T(8,128)(2,1)} custom-call(bf16[128,48,128]{2,1,0:T(8,128)(2,1)} %pack.1.packed), custom_call_target="tpu_custom_call" | custom-call | tf_op jit(solution)/shard_map/dispatch/pallas_call | solution.py:346
  87.4 17.9 %expert.1.made = bf16[4,128,48,128]{3,2,1,0:T(8,128)(2,1)} custom-call(bf16[4,128,48,128]{3,2,1,0:T(8,128)(2,1)} %dispatch.1.in_ref, bf16[1,384,2048]{2,1,0:T(8,128)(2,1)} %gate_ref.1, bf16[1,384,2048]{2,1,0:T(8,128)(2,1)} %up_ref.1, bf16[1,384,2048]{2,1,0:T(8,128)(2,1)} %down_ref.1), custom_call_target="tpu_custom_call" | custom-call | tf_op jit(solution)/shard_map/expert/pallas_call | solution.py:361
  105.3 0.0 copy-start
  105.3 0.0 copy-start.1
  105.3 82.5 %giveback.1.ret_ref = bf16[128,48,128]{2,1,0:T(8,128)(2,1)} custom-call(bf16[4,128,48,128]{3,2,1,0:T(8,128)(2,1)} %expert.1.made), custom_call_target="tpu_custom_call" | custom-call | tf_op jit(solution)/shard_map/giveback/pallas_call | solution.py:371
  187.8 0.0 copy-done
  187.9 0.7 copy.7.ids_ref
  188.6 0.0 copy-done.1
  188.6 0.7 copy.8.probs_ref
  189.3 5.6 %combine.1 = bf16[128,512]{1,0:T(8,128)(2,1)} custom-call(s32[128,8]{1,0:T(8,128)} %copy.7.ids_ref, f32[128,8]{1,0:T(8,128)} %copy.8.probs_ref, bf16[128,48,128]{2,1,0:T(8,128)(2,1)} %giveback.1.ret_ref), custom_call_target="tpu_custom_call" | custom-call | tf_op jit(solution)/shard_map/combine/pallas_call | solution.py:382
Async XLA Ops:
  105.3 82.5 %copy-start = (s32[128,8]{0,1:T(8,128)S(1)}, s32[128,8]{0,1:T(8,128)}, u32[]{:S(2)}) copy-start(s32[128,8]{0,1:T(8,128)} %param.7) | copy-start | bytes 12292
  105.3 83.3 %copy-start.1 = (f32[128,8]{0,1:T(8,128)S(1)}, f32[128,8]{0,1:T(8,128)}, u32[]{:S(2)}) copy-start(f32[128,8]{0,1:T(8,128)} %param.8) | copy-start | bytes 12292

commit v2 on v0

v2 whole, which is shorter than its diff:
```python
import functools

import jax
import jax.numpy as jnp
from jax import lax
from jax.experimental import pallas as pl
from jax.experimental.pallas import tpu as pltpu
from jax.sharding import PartitionSpec as P

LANES = 128
CAP = 12
TILE = 16
TILES = 3
ROWS = TILE * TILES
F32 = jnp.float32
BF16 = jnp.bfloat16


def wanted_slot(tile, row):
    return jnp.where(row < CAP, row, row - CAP + 4 * tile)


def grid_place(nz):
    e = lax.axis_index("expert")
    core = lax.rem(e, 2)
    z = lax.rem(lax.div(e, 2), nz)
    y = lax.div(e, 2 * nz)
    return e, y, z, core


def peer_of(k, sign, place, ny, nz):
    _, y, z, core = place
    group = lax.div(k, 2 * nz)
    item = lax.rem(k, 2 * nz)
    dz = lax.div(item, 2)
    dc = lax.rem(item, 2)
    dy = lax.rem(dz + group, ny)
    if sign > 0:
        y2, z2 = lax.rem(y + dy, ny), lax.rem(z + dz, nz)
    else:
        y2, z2 = lax.rem(y + ny - dy, ny), lax.rem(z + nz - dz, nz)
    return (y2 * nz + z2) * 2 + lax.rem(core + dc, 2)


def remote(src, dst, send, recv, device):
    return pltpu.make_async_remote_copy(
        src_ref=src,
        dst_ref=dst,
        send_sem=send,
        recv_sem=recv,
        device_id=device,
        device_id_type=pl.DeviceIdType.MESH,
    )


def side_of(x, way):
    return lax.rem(x + 1 + 2 * way, 4)


def route_tables(ids_ref, probs_ref, experts):
    top, tokens = ids_ref.shape
    probs = probs_ref[...]
    route = probs / jnp.sum(probs, axis=0, keepdims=True)
    which = lax.broadcasted_iota(jnp.int32, (experts, tokens), 0)
    chosen = jnp.zeros((experts, tokens), F32)
    weight = jnp.zeros((experts, tokens), F32)
    for k in range(top):
        hit = which == ids_ref[k : k + 1, :]
        chosen = chosen + hit.astype(F32)
        weight = weight + jnp.where(hit, route[k : k + 1, :], 0.0)
    before = lax.broadcasted_iota(jnp.int32, (tokens, tokens), 0)
    after = lax.broadcasted_iota(jnp.int32, (tokens, tokens), 1)
    upper = (before < after).astype(F32).astype(BF16)
    rank = jnp.dot(chosen.astype(BF16), upper, preferred_element_type=F32)
    return jnp.where(chosen > 0.0, rank, -1.0), weight


def pack(slot_ref, tok_ref, packed):
    experts, tokens = slot_ref.shape
    block = min(16, experts)
    row = lax.broadcasted_iota(jnp.int32, (block, TILE, tokens), 1)
    rows2 = lax.broadcasted_iota(jnp.int32, (block, TILE, LANES), 1)

    def step(i, carry):
        start = pl.multiple_of(i * block, block)
        mine = jnp.broadcast_to(slot_ref[pl.ds(start, block), :][:, None, :], (block, TILE, tokens))
        for tile in range(TILES):
            pick = (mine == wanted_slot(tile, row)).astype(F32).astype(BF16)
            pick = pick.reshape(block * TILE, tokens)
            source = jnp.concatenate(
                [tok_ref[:, tile * LANES : (tile + 1) * LANES], tok_ref[:, TILES * LANES :]], axis=1
            )
            got = jnp.dot(pick, source, preferred_element_type=F32)
            main = got[:, :LANES].reshape(block, TILE, LANES)
            rest = got[:, LANES:].reshape(block, TILE, LANES)
            packed[pl.ds(start, block), tile * TILE : (tile + 1) * TILE, :] = jnp.where(
                rows2 < CAP, main, rest
            ).astype(BF16)
        return carry

    lax.fori_loop(0, experts // block, step, 0)


def mixing(slot, weight, mix):
    tokens, experts = slot.shape
    high = weight.astype(BF16)
    rest = (weight - high.astype(F32)).astype(BF16)
    wide = experts * TILE
    column = lax.broadcasted_iota(jnp.int32, (experts, wide), 1)
    line = lax.broadcasted_iota(jnp.int32, (experts, wide), 0)
    spread = ((column >= line * TILE) & (column < line * TILE + TILE)).astype(F32).astype(BF16)
    slots = jnp.dot(slot.astype(BF16), spread, preferred_element_type=F32).astype(jnp.int32)
    highs = jnp.dot(high, spread, preferred_element_type=F32)
    rests = jnp.dot(rest, spread, preferred_element_type=F32)
    row = lax.broadcasted_iota(jnp.int32, (tokens, wide), 1) & (TILE - 1)
    for tile in range(TILES):
        hit = slots == wanted_slot(tile, row)
        masks = (hit & (row < CAP), hit & (row >= CAP))
        for i, (m, w) in enumerate((m, w) for m in masks for w in (highs, rests)):
            mix[tile, i * tokens : (i + 1) * tokens, :] = jnp.where(m, w, 0.0).astype(BF16)


def combine(mix, ret, out_ref):
    tokens = out_ref.shape[0]
    experts = ret.shape[0]
    last = jnp.zeros((tokens, LANES), F32)
    for tile in range(TILES):
        right = ret[:, tile * TILE : (tile + 1) * TILE, :].reshape(experts * TILE, LANES)
        got = jnp.dot(mix[tile], right, preferred_element_type=F32)
        out_ref[:, tile * LANES : (tile + 1) * LANES] = (
            got[:tokens] + got[tokens : 2 * tokens]
        ).astype(BF16)
        last = last + got[2 * tokens : 3 * tokens] + got[3 * tokens :]
    out_ref[:, TILES * LANES :] = last.astype(BF16)


def apply_expert(arrived, made, start, batch, rows_ref, gate_up, down):
    parts = arrived.shape[0]
    ff = down.shape[0]
    rows = batch * TILE
    half = TILE // 2
    low = lax.broadcasted_iota(jnp.int32, (batch, half, LANES), 1) < half // 2
    for q in range(parts):
        uppers = []
        base = q * (TILES + 1) * LANES
        for tile in range(TILES):
            value = arrived[q, pl.ds(start, batch), tile * TILE : (tile + 1) * TILE, :]
            rows_ref[:, base + tile * LANES : base + (tile + 1) * LANES] = value.reshape(rows, LANES)
            uppers.append(value.astype(F32)[:, half:, :])
        first = jnp.where(low, pltpu.roll(uppers[0], half // 2, 1), uppers[1])
        second = pltpu.roll(uppers[2], half // 2, 1)
        last = jnp.concatenate([first, second], axis=1).reshape(rows, LANES).astype(BF16)
        rows_ref[:, base + TILES * LANES : base + (TILES + 1) * LANES] = last
    dims = (((1,), (1,)), ((), ()))
    both = lax.dot_general(rows_ref[...], gate_up[...], dims, preferred_element_type=F32)
    gate, up = both[:, :ff], both[:, ff:]
    hidden = (gate / (1.0 + jnp.exp(-gate)) * up).astype(BF16)
    for q in range(parts):
        base = q * (TILES + 1) * LANES
        result = jnp.dot(
            hidden, down[:, base : base + (TILES + 1) * LANES], preferred_element_type=F32
        )
        last = result[:, TILES * LANES :].reshape(batch, TILE, LANES)
        fill = (
            pltpu.roll(last[:, :half], half // 2, 1),
            last[:, :half],
            pltpu.roll(last[:, half:], half // 2, 1),
        )
        for tile in range(TILES):
            main = result[:, tile * LANES : (tile + 1) * LANES].reshape(batch, TILE, LANES)
            upper = jnp.where(low, main[:, half:], fill[tile])
            made[q, pl.ds(start, batch), tile * TILE : (tile + 1) * TILE, :] = jnp.concatenate(
                [main[:, :half], upper], axis=1
            ).astype(BF16)


def moe_kernel(
    ny, nz, ids_ref, probs_ref, tok_ref, gate_hbm, up_hbm, down_hbm, out_ref,
    gate_up, down, slot_ref, packed, arrived, rows_ref, made, diag, near, passed, total, ret, mix,
    weight_sem, go_send, go_recv, gather_send, side_recv, far_recv,
    sum_send, diag_recv, near_recv, back_send, back_recv, self_sem,
):
    n = 2 * ny * nz
    per = 2 * nz
    ff = down.shape[0]
    x = lax.axis_index("dp")
    place = grid_place(nz)
    e = place[0]
    right, left, far = side_of(x, 0), side_of(x, 1), lax.rem(x + 2, 4)

    weights = (
        pltpu.make_async_copy(gate_hbm.at[0], gate_up.at[pl.ds(0, ff)], weight_sem.at[0]),
        pltpu.make_async_copy(up_hbm.at[0], gate_up.at[pl.ds(ff, ff)], weight_sem.at[1]),
        pltpu.make_async_copy(down_hbm.at[0], down, weight_sem.at[2]),
    )
    for copy in weights:
        copy.start()

    barrier = pltpu.get_barrier_semaphore()

    def greet(k, carry):
        pl.semaphore_signal(
            barrier,
            inc=1,
            device_id={"expert": peer_of(k, 1, place, ny, nz)},
            device_id_type=pl.DeviceIdType.MESH,
        )
        return carry

    for side in (right, left):
        pl.semaphore_signal(
            barrier, inc=1, device_id={"dp": side}, device_id_type=pl.DeviceIdType.MESH
        )
    lax.fori_loop(1, n, greet, 0)

    slot, weight = route_tables(ids_ref, probs_ref, n)
    slot_ref[...] = slot.astype(jnp.int32)
    pack(slot_ref, tok_ref, packed)
    pl.semaphore_wait(barrier, n + 1)

    def send_out(k, carry):
        dest = peer_of(k, 1, place, ny, nz)
        remote(
            packed.at[dest], arrived.at[x, k], go_send, go_recv.at[lax.div(k, per)], {"expert": dest}
        ).start()
        return carry

    own = pltpu.make_async_copy(packed.at[e], arrived.at[x, 0], self_sem.at[0])
    own.start()
    lax.fori_loop(1, n, send_out, 0)
    mixing(slot.T, weight.T, mix)
    for copy in weights:
        copy.wait()
    own.wait()

    def got(q, g):
        return arrived.at[q, pl.ds(g * per, per)]

    def part(q, g):
        return made.at[q, pl.ds(g * per, per)]

    def share(g):
        @pl.when(g == 0)
        def _():
            some = arrived.at[x, pl.ds(1, per - 1)]
            remote(some, some, go_send, go_recv.at[0], {"dp": right}).wait_recv()

        @pl.when(g > 0)
        def _():
            remote(got(x, g), got(x, g), go_send, go_recv.at[g], {"dp": right}).wait_recv()

        for way in (0, 1):
            remote(
                got(x, g), got(x, g), gather_send, side_recv.at[way, g], {"dp": side_of(x, way)}
            ).start()

    def share_on(g):
        way = lax.rem(g, 2)
        block = got(side_of(x, 1 - way), g)
        remote(block, block, gather_send, side_recv.at[way, g], {"dp": right}).wait_recv()
        remote(block, block, gather_send, far_recv.at[g], {"dp": side_of(x, way)}).start()

    def work(g):
        way = lax.rem(g, 2)
        block = got(side_of(x, way), g)
        remote(block, block, gather_send, side_recv.at[1 - way, g], {"dp": right}).wait_recv()
        remote(got(far, g), got(far, g), gather_send, far_recv.at[g], {"dp": right}).wait_recv()
        apply_expert(arrived, made, g * per, per, rows_ref, gate_up, down)
        remote(
            part(far, g), diag.at[g], sum_send, diag_recv.at[g], {"dp": side_of(x, way)}
        ).start()
        other = side_of(x, 1 - way)
        remote(
            part(other, g), near.at[1 - way, g], sum_send, near_recv.at[1 - way, g], {"dp": other}
        ).start()

    def sum_on(g):
        way = lax.rem(g, 2)
        dest = side_of(x, way)
        remote(diag.at[g], diag.at[g], sum_send, diag_recv.at[g], {"dp": right}).wait_recv()
        passed[g] = (
            diag[g].astype(F32) + made[dest, pl.ds(g * per, per)].astype(F32)
        ).astype(BF16)
        remote(
            passed.at[g], near.at[way, g], sum_send, near_recv.at[way, g], {"dp": dest}
        ).start()

    def give_back(g):
        for way in (0, 1):
            block = near.at[way, g]
            remote(block, block, sum_send, near_recv.at[way, g], {"dp": right}).wait_recv()
        total[g] = (
            made[x, pl.ds(g * per, per)].astype(F32)
            + near[0, g].astype(F32)
            + near[1, g].astype(F32)
        ).astype(BF16)

        def send(i, carry):
            dest = peer_of(g * per + i, -1, place, ny, nz)
            remote(total.at[g, i], ret.at[e], back_send, back_recv, {"expert": dest}).start()
            return carry

        @pl.when(g == 0)
        def _():
            pltpu.make_async_copy(total.at[0, 0], ret.at[e], self_sem.at[1]).start()
            lax.fori_loop(1, per, send, 0)

        @pl.when(g > 0)
        def _():
            lax.fori_loop(0, per, send, 0)

    def step(i, carry):
        for stage, late in ((share, 0), (share_on, 1), (sum_on, 3), (work, 2), (give_back, 4)):

            @pl.when((i >= late) & (i < ny + late))
            def _(stage=stage, late=late):
                stage(i - late)

        return carry

    lax.fori_loop(0, ny + 4, step, 0)
    pltpu.make_async_copy(total.at[0, 0], ret.at[e], self_sem.at[1]).wait()
    most = ret.at[pl.ds(0, n - 1)]
    remote(most, most, back_send, back_recv, {"dp": right}).wait_recv()
    combine(mix, ret, out_ref)
    remote(most, most, back_send, back_recv, {"dp": right}).wait_send()
    remote(most, most, go_send, back_recv, {"dp": right}).wait_send()
    three = made.at[pl.ds(0, 3)]
    remote(three, three, gather_send, back_recv, {"dp": right}).wait_send()
    remote(three, three, sum_send, back_recv, {"dp": right}).wait_send()


def local(ny, nz, tokens, expert_ids, chosen_probs, gate_weight, up_weight, down_weight):
    n = 2 * ny * nz
    per = 2 * nz
    count, ff, width = tokens.shape[0], gate_weight.shape[1], gate_weight.shape[2]
    dma = pltpu.SemaphoreType.DMA
    vmem = pl.BlockSpec(memory_space=pltpu.VMEM)
    anywhere = pl.BlockSpec(memory_space=pl.ANY)
    messages = (ROWS, LANES)
    return pl.pallas_call(
        functools.partial(moe_kernel, ny, nz),
        out_shape=jax.ShapeDtypeStruct(tokens.shape, BF16),
        in_specs=[vmem] * 3 + [anywhere] * 3,
        out_specs=vmem,
        scratch_shapes=[
            pltpu.VMEM((2 * ff, width), BF16),
            pltpu.VMEM((ff, width), BF16),
            pltpu.VMEM((n, count), jnp.int32),
            pltpu.VMEM((n,) + messages, BF16),
            pltpu.VMEM((4, n) + messages, BF16),
            pltpu.VMEM((per * TILE, width), BF16),
            pltpu.VMEM((4, n) + messages, BF16),
            pltpu.VMEM((ny, per) + messages, BF16),
            pltpu.VMEM((2, ny, per) + messages, BF16),
            pltpu.VMEM((ny, per) + messages, BF16),
            pltpu.VMEM((ny, per) + messages, BF16),
            pltpu.VMEM((n,) + messages, BF16),
            pltpu.VMEM((TILES, 4 * count, n * TILE), BF16),
            dma((3,)), dma(()), dma((ny,)), dma(()), dma((2, ny)), dma((ny,)),
            dma(()), dma((ny,)), dma((2, ny)), dma(()), dma(()), dma((2,)),
        ],
        compiler_params=pltpu.CompilerParams(
            collective_id=0, has_side_effects=True, vmem_limit_bytes=60 << 20
        ),
        name="moe",
    )(expert_ids.T, chosen_probs.T, tokens, gate_weight, up_weight, down_weight)


def build(mesh, ny, nz):
    in_specs = (
        P("expert", "dp"),
        P("expert", None),
        P("expert", None),
        P("expert", "dp", None),
        P("expert", "dp", None),
        P("expert", "dp", None),
    )
    return jax.shard_map(
        functools.partial(local, ny, nz),
        mesh=mesh,
        in_specs=in_specs,
        out_specs=P("expert", "dp"),
        check_vma=False,
    )


def solution(mesh):
    return build(mesh, 8, 8)
```

time: 669 us -> 152 us (0.23)
  waiting for transfers between devices: 289 us -> 0 us
  blocking collectives: 223 us -> 0 us
  Pallas kernels: 0 us -> 151 us
  local copies, waits for them, and re-layouts: 83.2 us -> 1.57 us
  matrix products: 23.1 us -> 0 us
  starting transfers between devices: 20.5 us -> 0 us
  between operations: 13.9 us -> 0.01 us
  other arithmetic: 10.4 us -> 0 us
    all_to_all x1 -> x0, waiting for transfers between devices: 225 us -> none  [local(): lax.all_to_all(produced, 'expert', split_axis=0, concat_axis=0, tiled=True)]
    all_to_all x1 -> x0, blocking collectives: 212 us -> none  [local(): lax.all_to_all(outgoing, 'expert', split_axis=0, concat_axis=0, tiled=True)]
    pallas_call x0 -> x1, Pallas kernels: none -> 151 us  [local(): pl.pallas_call(functools.partial(moe_kernel, ny, nz), out_shape=jax.Shape...]
    reduce_scatter x1 -> x0, waiting for transfers between devices: 63.8 us -> none  [local(): lax.psum_scatter(partial_out, 'dp', scatter_dimension=1, tiled=True)]
    scatter x1 -> x0, local copies, waits for them, and re-layouts: 34.5 us -> none  [local(): buffer = jnp.zeros((n_experts * capacity, columns_now), jnp.bfloat16).at[...]
    dot_general x2 -> x0, matrix products: 23.1 us -> none  [the longest x1 14.2 us: local(): jnp.einsum('snf,fd->snd', hidden, down_local, preferred_element_type=jnp....]
    reshape x2 -> x0, local copies, waits for them, and re-layouts: 21.5 us -> none  [the longest x1 10.9 us: local(): picked = returned.reshape(n_experts * capacity, width)[place]]
    all_to_all x1 -> x0, starting transfers between devices: 20.4 us -> none  [local(): lax.all_to_all(produced, 'expert', split_axis=0, concat_axis=0, tiled=True)]
  transfers between devices with their start and end apart: 2 -> 0, of which waited for: 2 -> 0; matrix products, arithmetic and copies ran while one was open for 0% -> 0% of each run, Pallas kernels for 0% -> 0%
where the time goes in v2:
time: 152 us
  Pallas kernels  151 us (99%)
  local copies, waits for them, and re-layouts  1.57 us (1%)
    pallas_call x1, Pallas kernels, local(): pl.pallas_call(functools.partial(moe_kernel, ny, nz), out_shape=jax.Shape...  151 us

profile of v2, /device:TPU:1, one launch (start us, length us, event | category | flops | bytes accessed | tf_op | source)
XLA Modules:
  0.0 152.3 jit_solution(13185143581976928137)
XLA Ops:
  0.0 150.7 %moe.1 = bf16[128,512]{1,0:T(8,128)(2,1)} custom-call(s32[8,128]{1,0:T(8,128)} %bitcast.2, f32[8,128]{1,0:T(8,128)} %bitcast.3, bf16[128,512]{1,0:T(8,128)(2,1)} %tok_ref.1, bf16[1,384,2048]{2,1,0:T(8,128)(2,1)} %gate_hbm.1, bf16[1,384,2048]{2,1,0:T(8,128)(2,1)} %up_hbm.1, bf16[1,384,2048]{2,1,0:T(8,128)(2,1)} %down_hbm.1), custom_call_target="tpu_custom_call" | custom-call | tf_op jit(solution)/shard_map/moe/pallas_call | solution.py:341
  150.7 1.6 %copy.8 = bf16[128,512]{1,0:T(8,128)(2,1)} copy(bf16[128,512]{1,0:T(8,128)(2,1)} %moe.1) | data formatting | bytes 262144

commit v3 on v2

--- a/solution.py
+++ b/solution.py
@@ -28,18 +28,35 @@
     return e, y, z, core
 
 
-def peer_of(k, sign, place, ny, nz):
+def peer_at(ring, half, j, dc, sign, place, ny, nz):
     _, y, z, core = place
-    group = lax.div(k, 2 * nz)
-    item = lax.rem(k, 2 * nz)
-    dz = lax.div(item, 2)
-    dc = lax.rem(item, 2)
-    dy = lax.rem(dz + group, ny)
+    dz = j + half * (nz // 2)
     if sign > 0:
-        y2, z2 = lax.rem(y + dy, ny), lax.rem(z + dz, nz)
+        y2, z2 = lax.rem(y + dz + ring, ny), lax.rem(z + dz, nz)
     else:
-        y2, z2 = lax.rem(y + ny - dy, ny), lax.rem(z + nz - dz, nz)
+        y2, z2 = lax.rem(y + 2 * ny - lax.rem(dz + ring, ny), ny), lax.rem(z + nz - dz, nz)
     return (y2 * nz + z2) * 2 + lax.rem(core + dc, 2)
+
+
+def for_peers(ring, half, place, ny, nz, sign, act):
+    for j in range(nz // 2):
+        for dc in range(2):
+            act(2 * j + dc, peer_at(ring, half, j, dc, sign, place, ny, nz))
+
+
+def group_of(g):
+    ring = lax.div(g, 2)
+    return ring, lax.rem(g + ring, 2)
+
+
+def column_experts(place, ny, nz, wide):
+    _, y, z, core = place
+    k = lax.broadcasted_iota(jnp.int32, (1, wide), 1) >> 4
+    g = k >> (nz.bit_length() - 1)
+    ring = g >> 1
+    dz = ((k & (nz - 1)) >> 1) + (((g + ring) & 1) << (nz.bit_length() - 2))
+    y2, z2 = (y + dz + ring) & (ny - 1), (z + dz) & (nz - 1)
+    return (y2 * nz + z2) * 2 + ((core + k) & 1)
 
 
 def remote(src, dst, send, recv, device):
@@ -101,14 +118,13 @@
     lax.fori_loop(0, experts // block, step, 0)
 
 
-def mixing(slot, weight, mix):
+def mixing(slot, weight, columns, mix):
     tokens, experts = slot.shape
     high = weight.astype(BF16)
     rest = (weight - high.astype(F32)).astype(BF16)
     wide = experts * TILE
-    column = lax.broadcasted_iota(jnp.int32, (experts, wide), 1)
     line = lax.broadcasted_iota(jnp.int32, (experts, wide), 0)
-    spread = ((column >= line * TILE) & (column < line * TILE + TILE)).astype(F32).astype(BF16)
+    spread = (line == columns).astype(F32).astype(BF16)
     slots = jnp.dot(slot.astype(BF16), spread, preferred_element_type=F32).astype(jnp.int32)
     highs = jnp.dot(high, spread, preferred_element_type=F32)
     rests = jnp.dot(rest, spread, preferred_element_type=F32)
@@ -120,18 +136,21 @@
             mix[tile, i * tokens : (i + 1) * tokens, :] = jnp.where(m, w, 0.0).astype(BF16)
 
 
-def combine(mix, ret, out_ref):
-    tokens = out_ref.shape[0]
-    experts = ret.shape[0]
-    last = jnp.zeros((tokens, LANES), F32)
+def combine(mix, ret, start, stop, before):
+    tokens = mix.shape[1] // 4
+    sums = []
+    last = None
     for tile in range(TILES):
-        right = ret[:, tile * TILE : (tile + 1) * TILE, :].reshape(experts * TILE, LANES)
-        got = jnp.dot(mix[tile], right, preferred_element_type=F32)
-        out_ref[:, tile * LANES : (tile + 1) * LANES] = (
-            got[:tokens] + got[tokens : 2 * tokens]
-        ).astype(BF16)
-        last = last + got[2 * tokens : 3 * tokens] + got[3 * tokens :]
-    out_ref[:, TILES * LANES :] = last.astype(BF16)
+        right = ret[start:stop, tile * TILE : (tile + 1) * TILE, :]
+        right = right.reshape((stop - start) * TILE, LANES)
+        got = jnp.dot(
+            mix[tile, :, start * TILE : stop * TILE], right, preferred_element_type=F32
+        )
+        sums.append(got[:tokens] + got[tokens : 2 * tokens])
+        more = got[2 * tokens : 3 * tokens] + got[3 * tokens :]
+        last = more if last is None else last + more
+    sums.append(last)
+    return [a + b for a, b in zip(before, sums)] if before else sums
 
 
 def apply_expert(arrived, made, start, batch, rows_ref, gate_up, down):
@@ -181,7 +200,8 @@
     sum_send, diag_recv, near_recv, back_send, back_recv, self_sem,
 ):
     n = 2 * ny * nz
-    per = 2 * nz
+    per = nz
+    groups = n // per
     ff = down.shape[0]
     x = lax.axis_index("dp")
     place = grid_place(nz)
@@ -198,37 +218,58 @@
 
     barrier = pltpu.get_barrier_semaphore()
 
-    def greet(k, carry):
-        pl.semaphore_signal(
-            barrier,
-            inc=1,
-            device_id={"expert": peer_of(k, 1, place, ny, nz)},
-            device_id_type=pl.DeviceIdType.MESH,
-        )
+    def greet(g, carry):
+        def act(i, dest):
+            def signal():
+                pl.semaphore_signal(
+                    barrier,
+                    inc=1,
+                    device_id={"expert": dest},
+                    device_id_type=pl.DeviceIdType.MESH,
+                )
+
+            if i == 0:
+                pl.when(g > 0)(signal)
+            else:
+                signal()
+
+        for_peers(*group_of(g), place, ny, nz, 1, act)
         return carry
 
     for side in (right, left):
         pl.semaphore_signal(
             barrier, inc=1, device_id={"dp": side}, device_id_type=pl.DeviceIdType.MESH
         )
-    lax.fori_loop(1, n, greet, 0)
+    lax.fori_loop(0, groups, greet, 0)
 
     slot, weight = route_tables(ids_ref, probs_ref, n)
     slot_ref[...] = slot.astype(jnp.int32)
     pack(slot_ref, tok_ref, packed)
     pl.semaphore_wait(barrier, n + 1)
 
-    def send_out(k, carry):
-        dest = peer_of(k, 1, place, ny, nz)
-        remote(
-            packed.at[dest], arrived.at[x, k], go_send, go_recv.at[lax.div(k, per)], {"expert": dest}
-        ).start()
+    def send_out(g, carry):
+        def act(i, dest):
+            def start():
+                remote(
+                    packed.at[dest],
+                    arrived.at[x, g * per + i],
+                    go_send,
+                    go_recv.at[g],
+                    {"expert": dest},
+                ).start()
+
+            if i == 0:
+                pl.when(g > 0)(start)
+            else:
+                start()
+
+        for_peers(*group_of(g), place, ny, nz, 1, act)
         return carry
 
     own = pltpu.make_async_copy(packed.at[e], arrived.at[x, 0], self_sem.at[0])
     own.start()
-    lax.fori_loop(1, n, send_out, 0)
-    mixing(slot.T, weight.T, mix)
+    lax.fori_loop(0, groups, send_out, 0)
+    mixing(slot.T, weight.T, column_experts(place, ny, nz, n * TILE), mix)
     for copy in weights:
         copy.wait()
     own.wait()
@@ -295,44 +336,56 @@
             + near[1, g].astype(F32)
         ).astype(BF16)
 
-        def send(i, carry):
-            dest = peer_of(g * per + i, -1, place, ny, nz)
-            remote(total.at[g, i], ret.at[e], back_send, back_recv, {"expert": dest}).start()
-            return carry
+        def act(i, dest):
+            def start():
+                remote(
+                    total.at[g, i], ret.at[g * per + i], back_send, back_recv.at[g], {"expert": dest}
+                ).start()
+
+            if i == 0:
+                pl.when(g > 0)(start)
+            else:
+                start()
+
+        for_peers(*group_of(g), place, ny, nz, -1, act)
 
         @pl.when(g == 0)
         def _():
-            pltpu.make_async_copy(total.at[0, 0], ret.at[e], self_sem.at[1]).start()
-            lax.fori_loop(1, per, send, 0)
-
-        @pl.when(g > 0)
-        def _():
-            lax.fori_loop(0, per, send, 0)
+            pltpu.make_async_copy(total.at[0, 0], ret.at[0], self_sem.at[1]).start()
 
     def step(i, carry):
         for stage, late in ((share, 0), (share_on, 1), (sum_on, 3), (work, 2), (give_back, 4)):
 
-            @pl.when((i >= late) & (i < ny + late))
+            @pl.when((i >= late) & (i < groups + late))
             def _(stage=stage, late=late):
                 stage(i - late)
 
         return carry
 
-    lax.fori_loop(0, ny + 4, step, 0)
-    pltpu.make_async_copy(total.at[0, 0], ret.at[e], self_sem.at[1]).wait()
+    lax.fori_loop(0, groups + 4, step, 0)
+    pltpu.make_async_copy(total.at[0, 0], ret.at[0], self_sem.at[1]).wait()
+    early = groups - max(1, groups // 4)
+    sums = None
+    for start, stop in ((0, early), (early, groups)):
+        for g in range(start, stop):
+            first = 1 if g == 0 else 0
+            block = ret.at[pl.ds(g * per + first, per - first)]
+            remote(block, block, back_send, back_recv.at[g], {"dp": right}).wait_recv()
+        sums = combine(mix, ret, start * per, stop * per, sums)
+    for chunk, value in enumerate(sums):
+        out_ref[:, chunk * LANES : (chunk + 1) * LANES] = value.astype(BF16)
     most = ret.at[pl.ds(0, n - 1)]
-    remote(most, most, back_send, back_recv, {"dp": right}).wait_recv()
-    combine(mix, ret, out_ref)
-    remote(most, most, back_send, back_recv, {"dp": right}).wait_send()
-    remote(most, most, go_send, back_recv, {"dp": right}).wait_send()
+    remote(most, most, back_send, go_recv.at[0], {"dp": right}).wait_send()
+    remote(most, most, go_send, go_recv.at[0], {"dp": right}).wait_send()
     three = made.at[pl.ds(0, 3)]
-    remote(three, three, gather_send, back_recv, {"dp": right}).wait_send()
-    remote(three, three, sum_send, back_recv, {"dp": right}).wait_send()
+    remote(three, three, gather_send, go_recv.at[0], {"dp": right}).wait_send()
+    remote(three, three, sum_send, go_recv.at[0], {"dp": right}).wait_send()
 
 
 def local(ny, nz, tokens, expert_ids, chosen_probs, gate_weight, up_weight, down_weight):
     n = 2 * ny * nz
-    per = 2 * nz
+    per = nz
+    groups = n // per
     count, ff, width = tokens.shape[0], gate_weight.shape[1], gate_weight.shape[2]
     dma = pltpu.SemaphoreType.DMA
     vmem = pl.BlockSpec(memory_space=pltpu.VMEM)
@@ -351,14 +404,14 @@
             pltpu.VMEM((4, n) + messages, BF16),
             pltpu.VMEM((per * TILE, width), BF16),
             pltpu.VMEM((4, n) + messages, BF16),
-            pltpu.VMEM((ny, per) + messages, BF16),
-            pltpu.VMEM((2, ny, per) + messages, BF16),
-            pltpu.VMEM((ny, per) + messages, BF16),
-            pltpu.VMEM((ny, per) + messages, BF16),
+            pltpu.VMEM((groups, per) + messages, BF16),
+            pltpu.VMEM((2, groups, per) + messages, BF16),
+            pltpu.VMEM((groups, per) + messages, BF16),
+            pltpu.VMEM((groups, per) + messages, BF16),
             pltpu.VMEM((n,) + messages, BF16),
             pltpu.VMEM((TILES, 4 * count, n * TILE), BF16),
-            dma((3,)), dma(()), dma((ny,)), dma(()), dma((2, ny)), dma((ny,)),
-            dma(()), dma((ny,)), dma((2, ny)), dma(()), dma(()), dma((2,)),
+            dma((3,)), dma(()), dma((groups,)), dma(()), dma((2, groups)), dma((groups,)),
+            dma(()), dma((groups,)), dma((2, groups)), dma(()), dma((groups,)), dma((2,)),
         ],
         compiler_params=pltpu.CompilerParams(
             collective_id=0, has_side_effects=True, vmem_limit_bytes=60 << 20

time: 152 us -> 155 us (1.020); the launches traced: 152 us -> 153 us
  no operation moved by 1% of the time
where the time goes in v3:
time: 155 us; the launch traced here: 153 us
  Pallas kernels  151 us (97%)
  local copies, waits for them, and re-layouts  1.57 us (1%)
    pallas_call x1, Pallas kernels, local(): pl.pallas_call(functools.partial(moe_kernel, ny, nz), out_shape=jax.Shape...  151 us

profile of v3, /device:TPU:1, one launch (start us, length us, event | category | flops | bytes accessed | tf_op | source)
XLA Modules:
  0.0 152.9 jit_solution(17630782608350408238)
XLA Ops:
  0.0 151.3 %moe.1 = bf16[128,512]{1,0:T(8,128)(2,1)} custom-call(s32[8,128]{1,0:T(8,128)} %bitcast.2, f32[8,128]{1,0:T(8,128)} %bitcast.3, bf16[128,512]{1,0:T(8,128)(2,1)} %tok_ref.1, bf16[1,384,2048]{2,1,0:T(8,128)(2,1)} %gate_hbm.1, bf16[1,384,2048]{2,1,0:T(8,128)(2,1)} %up_hbm.1, bf16[1,384,2048]{2,1,0:T(8,128)(2,1)} %down_hbm.1), custom_call_target="tpu_custom_call" | custom-call | tf_op jit(solution)/shard_map/moe/pallas_call | solution.py:394
  151.4 1.6 %copy.8 = bf16[128,512]{1,0:T(8,128)(2,1)} copy(bf16[128,512]{1,0:T(8,128)(2,1)} %moe.1) | data formatting | bytes 262144

commit v4 on v3

--- a/solution.py
+++ b/solution.py
@@ -30,7 +30,7 @@
 
 def peer_at(ring, half, j, dc, sign, place, ny, nz):
     _, y, z, core = place
-    dz = j + half * (nz // 2)
+    dz = 2 * j + half
     if sign > 0:
         y2, z2 = lax.rem(y + dz + ring, ny), lax.rem(z + dz, nz)
     else:
@@ -44,6 +44,14 @@
             act(2 * j + dc, peer_at(ring, half, j, dc, sign, place, ny, nz))
 
 
+def straight(g):
+    return lax.rem(lax.div(g, 2), 2) == 1
+
+
+def straight_index(g):
+    return 2 * lax.div(g, 4) + lax.rem(g, 2)
+
+
 def group_of(g):
     ring = lax.div(g, 2)
     return ring, lax.rem(g + ring, 2)
@@ -54,7 +62,7 @@
     k = lax.broadcasted_iota(jnp.int32, (1, wide), 1) >> 4
     g = k >> (nz.bit_length() - 1)
     ring = g >> 1
-    dz = ((k & (nz - 1)) >> 1) + (((g + ring) & 1) << (nz.bit_length() - 2))
+    dz = (k & (nz - 2)) + ((g + ring) & 1)
     y2, z2 = (y + dz + ring) & (ny - 1), (z + dz) & (nz - 1)
     return (y2 * nz + z2) * 2 + ((core + k) & 1)
 
@@ -196,12 +204,15 @@
 def moe_kernel(
     ny, nz, ids_ref, probs_ref, tok_ref, gate_hbm, up_hbm, down_hbm, out_ref,
     gate_up, down, slot_ref, packed, arrived, rows_ref, made, diag, near, passed, total, ret, mix,
+    far_tok, far_slot, far_packed, route_ref,
     weight_sem, go_send, go_recv, gather_send, side_recv, far_recv,
     sum_send, diag_recv, near_recv, back_send, back_recv, self_sem,
+    tok_send, tok_recv, straight_send, relay, relay_recv,
 ):
     n = 2 * ny * nz
     per = nz
     groups = n // per
+    direct = sum(g // 2 % 2 for g in range(groups))
     ff = down.shape[0]
     x = lax.axis_index("dp")
     place = grid_place(nz)
@@ -236,7 +247,7 @@
         for_peers(*group_of(g), place, ny, nz, 1, act)
         return carry
 
-    for side in (right, left):
+    for side in (right, left, far):
         pl.semaphore_signal(
             barrier, inc=1, device_id={"dp": side}, device_id_type=pl.DeviceIdType.MESH
         )
@@ -245,9 +256,19 @@
     slot, weight = route_tables(ids_ref, probs_ref, n)
     slot_ref[...] = slot.astype(jnp.int32)
     pack(slot_ref, tok_ref, packed)
-    pl.semaphore_wait(barrier, n + 1)
-
-    def send_out(g, carry):
+    pl.semaphore_wait(barrier, n + 2)
+    half = tok_ref.shape[0] // 2
+    for way in (0, 1):
+        remote(
+            tok_ref.at[pl.ds(way * half, half)],
+            relay.at[way],
+            tok_send,
+            relay_recv.at[way],
+            {"dp": side_of(x, way)},
+        ).start()
+    ahead = min(6, groups)
+
+    def send_out(g):
         def act(i, dest):
             def start():
                 remote(
@@ -264,15 +285,57 @@
                 start()
 
         for_peers(*group_of(g), place, ny, nz, 1, act)
-        return carry
+
+    def send_straight(g):
+        first = straight_index(g) * per
+
+        def act(i, dest):
+            remote(
+                far_packed.at[first + i],
+                arrived.at[far, g * per + i],
+                straight_send,
+                far_recv.at[g],
+                {"expert": dest},
+            ).start()
+
+        for_peers(*group_of(g), place, ny, nz, 1, act)
+
+    def pack_far():
+        def take(h, carry):
+            g = 4 * lax.div(h, 2) + 2 + lax.rem(h, 2)
+
+            def act(i, dest):
+                far_slot[pl.ds(h * per + i, 1), :] = slot_ref[pl.ds(dest, 1), :]
+
+            for_peers(*group_of(g), place, ny, nz, 1, act)
+            return carry
+
+        lax.fori_loop(0, direct, take, 0)
+        remote(far_tok, far_tok, tok_send, tok_recv, {"dp": right}).wait_recv()
+        pack(far_slot, far_tok, far_packed)
 
     own = pltpu.make_async_copy(packed.at[e], arrived.at[x, 0], self_sem.at[0])
     own.start()
-    lax.fori_loop(0, groups, send_out, 0)
-    mixing(slot.T, weight.T, column_experts(place, ny, nz, n * TILE), mix)
-    for copy in weights:
-        copy.wait()
+
+    def first_out(g, carry):
+        send_out(g)
+        return carry
+
+    lax.fori_loop(0, ahead, first_out, 0)
+    for way in (0, 1):
+        passing = remote(
+            relay.at[way],
+            far_tok.at[pl.ds(way * half, half)],
+            tok_send,
+            tok_recv,
+            {"dp": side_of(x, way)},
+        )
+        remote(relay.at[way], relay.at[way], tok_send, relay_recv.at[way], {"dp": right}).wait_recv()
+        passing.start()
+    route_ref[0] = slot.T
+    route_ref[1] = weight.T
     own.wait()
+    pack_far()
 
     def got(q, g):
         return arrived.at[q, pl.ds(g * per, per)]
@@ -299,7 +362,10 @@
         way = lax.rem(g, 2)
         block = got(side_of(x, 1 - way), g)
         remote(block, block, gather_send, side_recv.at[way, g], {"dp": right}).wait_recv()
-        remote(block, block, gather_send, far_recv.at[g], {"dp": side_of(x, way)}).start()
+
+        @pl.when(jnp.logical_not(straight(g)))
+        def _():
+            remote(block, block, gather_send, far_recv.at[g], {"dp": side_of(x, way)}).start()
 
     def work(g):
         way = lax.rem(g, 2)
@@ -353,8 +419,20 @@
         def _():
             pltpu.make_async_copy(total.at[0, 0], ret.at[0], self_sem.at[1]).start()
 
-    def step(i, carry):
-        for stage, late in ((share, 0), (share_on, 1), (sum_on, 3), (work, 2), (give_back, 4)):
+    def step(stages, i, carry):
+        @pl.when(i < groups)
+        def _():
+            share(i)
+
+        @pl.when(i < groups - ahead)
+        def _():
+            send_out(i + ahead)
+
+        @pl.when((i < groups - 2) & straight(i + 2))
+        def _():
+            send_straight(i + 2)
+
+        for stage, late in stages:
 
             @pl.when((i >= late) & (i < groups + late))
             def _(stage=stage, late=late):
@@ -362,7 +440,13 @@
 
         return carry
 
-    lax.fori_loop(0, groups + 4, step, 0)
+    first = ((share_on, 1),)
+    every = ((share_on, 1), (sum_on, 6), (work, 4), (give_back, 8))
+    lax.fori_loop(0, 4, functools.partial(step, first), 0)
+    mixing(route_ref[0], route_ref[1], column_experts(place, ny, nz, n * TILE), mix)
+    for copy in weights:
+        copy.wait()
+    lax.fori_loop(4, groups + 8, functools.partial(step, every), 0)
     pltpu.make_async_copy(total.at[0, 0], ret.at[0], self_sem.at[1]).wait()
     early = groups - max(1, groups // 4)
     sums = None
@@ -377,8 +461,15 @@
     most = ret.at[pl.ds(0, n - 1)]
     remote(most, most, back_send, go_recv.at[0], {"dp": right}).wait_send()
     remote(most, most, go_send, go_recv.at[0], {"dp": right}).wait_send()
+    for _ in (0, 1):
+        remote(far_tok, far_tok, tok_send, tok_recv, {"dp": right}).wait_send()
+    some = packed.at[pl.ds(0, direct * per)]
+    remote(some, some, straight_send, go_recv.at[0], {"dp": right}).wait_send()
+    some = packed.at[pl.ds(0, n - direct * per)]
+    remote(some, some, gather_send, go_recv.at[0], {"dp": right}).wait_send()
+    two = made.at[pl.ds(0, 2)]
+    remote(two, two, gather_send, go_recv.at[0], {"dp": right}).wait_send()
     three = made.at[pl.ds(0, 3)]
-    remote(three, three, gather_send, go_recv.at[0], {"dp": right}).wait_send()
     remote(three, three, sum_send, go_recv.at[0], {"dp": right}).wait_send()
 
 
@@ -386,6 +477,7 @@
     n = 2 * ny * nz
     per = nz
     groups = n // per
+    direct = sum(g // 2 % 2 for g in range(groups))
     count, ff, width = tokens.shape[0], gate_weight.shape[1], gate_weight.shape[2]
     dma = pltpu.SemaphoreType.DMA
     vmem = pl.BlockSpec(memory_space=pltpu.VMEM)
@@ -410,8 +502,14 @@
             pltpu.VMEM((groups, per) + messages, BF16),
             pltpu.VMEM((n,) + messages, BF16),
             pltpu.VMEM((TILES, 4 * count, n * TILE), BF16),
+            pltpu.VMEM(tokens.shape, BF16),
+            pltpu.VMEM((direct * per, count), jnp.int32),
+            pltpu.VMEM((direct * per,) + messages, BF16),
+            pltpu.VMEM((2, count, n), F32),
             dma((3,)), dma(()), dma((groups,)), dma(()), dma((2, groups)), dma((groups,)),
             dma(()), dma((groups,)), dma((2, groups)), dma(()), dma((groups,)), dma((2,)),
+            dma(()), dma(()), dma(()),
+            pltpu.VMEM((2, count // 2, tokens.shape[1]), BF16), dma((2,)),
         ],
         compiler_params=pltpu.CompilerParams(
             collective_id=0, has_side_effects=True, vmem_limit_bytes=60 << 20

time: 155 us -> 141 us (0.910)
  Pallas kernels: 151 us -> 139 us
    pallas_call x1, Pallas kernels: 151 us -> 139 us  [local(): pl.pallas_call(functools.partial(moe_kernel, ny, nz), out_shape=jax.Shape...]
where the time goes in v4:
time: 141 us; the launch traced here: 140 us
  Pallas kernels  139 us (99%)
  local copies, waits for them, and re-layouts  1.57 us (1%)
    pallas_call x1, Pallas kernels, local(): pl.pallas_call(functools.partial(moe_kernel, ny, nz), out_shape=jax.Shape...  139 us

profile of v4, /device:TPU:1, one launch (start us, length us, event | category | flops | bytes accessed | tf_op | source)
XLA Modules:
  0.0 140.2 jit_solution(6540061022884876970)
XLA Ops:
  0.0 138.6 %moe.1 = bf16[128,512]{1,0:T(8,128)(2,1)} custom-call(s32[8,128]{1,0:T(8,128)} %bitcast.2, f32[8,128]{1,0:T(8,128)} %bitcast.3, bf16[128,512]{1,0:T(8,128)(2,1)} %tok_ref.1, bf16[1,384,2048]{2,1,0:T(8,128)(2,1)} %gate_hbm.1, bf16[1,384,2048]{2,1,0:T(8,128)(2,1)} %up_hbm.1, bf16[1,384,2048]{2,1,0:T(8,128)(2,1)} %down_hbm.1), custom_call_target="tpu_custom_call" | custom-call | tf_op jit(solution)/shard_map/moe/pallas_call | solution.py:486
  138.6 1.6 %copy.8 = bf16[128,512]{1,0:T(8,128)(2,1)} copy(bf16[128,512]{1,0:T(8,128)(2,1)} %moe.1) | data formatting | bytes 262144

commit v5 on v4

--- a/solution.py
+++ b/solution.py
@@ -266,7 +266,7 @@
             relay_recv.at[way],
             {"dp": side_of(x, way)},
         ).start()
-    ahead = min(6, groups)
+    ahead = min(4, groups)
 
     def send_out(g):
         def act(i, dest):

time: 141 us -> 140 us (level)
  no operation moved by 1% of the time
where the time goes in v5:
time: 140 us
  Pallas kernels  138 us (99%)
  local copies, waits for them, and re-layouts  1.57 us (1%)
    pallas_call x1, Pallas kernels, local(): pl.pallas_call(functools.partial(moe_kernel, ny, nz), out_shape=jax.Shape...  138 us

profile of v5, /device:TPU:1, one launch (start us, length us, event | category | flops | bytes accessed | tf_op | source)
XLA Modules:
  0.0 139.7 jit_solution(3480749068380507734)
XLA Ops:
  0.0 138.1 %moe.1 = bf16[128,512]{1,0:T(8,128)(2,1)} custom-call(s32[8,128]{1,0:T(8,128)} %bitcast.2, f32[8,128]{1,0:T(8,128)} %bitcast.3, bf16[128,512]{1,0:T(8,128)(2,1)} %tok_ref.1, bf16[1,384,2048]{2,1,0:T(8,128)(2,1)} %gate_hbm.1, bf16[1,384,2048]{2,1,0:T(8,128)(2,1)} %up_hbm.1, bf16[1,384,2048]{2,1,0:T(8,128)(2,1)} %down_hbm.1), custom_call_target="tpu_custom_call" | custom-call | tf_op jit(solution)/shard_map/moe/pallas_call | solution.py:486
  138.1 1.6 %copy.8 = bf16[128,512]{1,0:T(8,128)(2,1)} copy(bf16[128,512]{1,0:T(8,128)(2,1)} %moe.1) | data formatting | bytes 262144
